TPU v7x, 32 devices: a whole 2x2x4 slice. The times are simulated.
32 devices in a mesh: group: 4 (over y, x), shard: 8 (over z, core).
Axes of the slice: x: 2, y: 2, z: 4, core: 2. Of those that a mesh axis runs over, the one named last changes fastest.
Arguments:
- queries: float32 [256, 768], P(('group', 'shard')), may hold values from -6 to 6
- codebook: float32 [96, 256, 8], replicated, may hold values from -0.21875 to 0.21875
- pq_codes: int32 [256, 96, 256], P(('group', 'shard')), may hold values from 0 to 255
- probes: int32 [256, 8], P('group'), may hold values from 0 to 63, all different within a row
- vectors: float32 [32768, 768], P(('group', 'shard')), may hold values from -0.21875 to 0.21875
- cand_owner: int32 [256, 16], P(('group', 'shard')), may hold values from 0 to 31, all different within a row; in each aligned block of 8 rows (0 to 7, 8 to 15, ...) at most 4 rows name the same one
- cand_row: int32 [256, 16], P(('group', 'shard')), may hold values from 0 to 1023
Outputs:
- pq_scores: float32 [256, 256, 64], P(('group', 'shard'))
- rerank_scores: float32 [256, 16], P(('group', 'shard'))
Inputs may be any that keep to these rules, and one draw needn't show every extreme that they name: The 8 probes of one query are distinct. `cand_owner`: the 16 owners of one query are distinct. Among the queries of one device no owner appears more than 4 times, and some owner appears exactly 4 times.
All inputs are finite; a program needn't handle non-finite values.
Results may differ from a plain program's by a relative error of at most 0.0029.
Values may be sent and summed in bfloat16 or wider, within the bound.
No kernel may reach another device: no remote copies, remote signals or barrier semaphores. Data moves between devices by JAX's collectives and lax.ppermute only.
A program may use at most 128 MiB of HBM per device.

v0:
```python
import jax
import jax.numpy as jnp
from jax import lax
from jax.sharding import PartitionSpec as P

M = 96
DS = 8
KS = 256


def build_tables(query_rows, codebook):
    number = query_rows.shape[0]
    pieces = query_rows.reshape(number, M, DS)
    tables = jnp.einsum("qmd,mkd->qmk", pieces, codebook, precision=lax.Precision.HIGHEST)
    return tables.reshape(number, M * KS).astype(jnp.bfloat16)


def score_lists(pq_codes, group_tables, probes, first_list):
    centres = jnp.arange(KS, dtype=jnp.int32)

    def one_list(inputs):
        list_codes, list_id = inputs
        onehot = (list_codes[:, None, :] == centres[None, :, None]).astype(jnp.bfloat16)
        onehot = onehot.reshape(M * KS, list_codes.shape[1])
        scores = lax.dot_general(
            onehot, group_tables, (((0,), (1,)), ((), ())), preferred_element_type=jnp.float32
        )
        probed = jnp.any(probes == list_id, axis=1)
        return jnp.where(probed[None, :], scores, 0.0)

    list_ids = first_list + jnp.arange(pq_codes.shape[0], dtype=jnp.int32)
    return lax.map(one_list, (pq_codes, list_ids))


def rerank(queries, vectors, cand_owner, cand_row):
    owners = lax.axis_size("group") * lax.axis_size("shard")
    pair_count = cand_owner.shape[0] * cand_owner.shape[1]
    capacity = max(2, pair_count // owners)
    owner_flat = cand_owner.reshape(pair_count)
    matches = (owner_flat[:, None] == jnp.arange(owners, dtype=jnp.int32)[None, :]).astype(
        jnp.int32
    )
    before = jnp.cumsum(matches, axis=0) - matches
    position = jnp.sum(before * matches, axis=1)
    target = owner_flat * capacity + position
    source = jnp.arange(pair_count, dtype=jnp.int32) // cand_owner.shape[1]
    send_rows = (
        jnp.zeros((owners * capacity, queries.shape[1]), jnp.float32)
        .at[target]
        .set(queries[source])
    )
    send_rows = send_rows.reshape(owners, capacity, queries.shape[1])
    send_ids = (
        jnp.full((owners * capacity,), -1.0, jnp.float32)
        .at[target]
        .set(cand_row.reshape(pair_count).astype(jnp.float32))
    )
    send_ids = send_ids.reshape(owners, capacity)
    rows_in = lax.all_to_all(send_rows, ("group", "shard"), split_axis=0, concat_axis=0, tiled=True)
    row_ids = lax.all_to_all(send_ids, ("group", "shard"), split_axis=0, concat_axis=0, tiled=True)
    filled = row_ids >= 0.0
    lookup = jnp.maximum(row_ids, 0.0).astype(jnp.int32)
    found = vectors[lookup]
    inner = jnp.einsum("snd,snd->sn", rows_in, found, precision=lax.Precision.HIGHEST)
    scored = jnp.where(filled, inner, 0.0)
    returned = lax.all_to_all(scored, ("group", "shard"), split_axis=0, concat_axis=0, tiled=True)
    result = returned.reshape(owners * capacity)[target]
    return result.reshape(cand_owner.shape)


def per_device(queries, codebook, pq_codes, probes, vectors, cand_owner, cand_row):
    first_list = lax.axis_index("shard") * pq_codes.shape[0]
    group_queries = lax.all_gather(queries, "shard", axis=0, tiled=True)
    group_tables = build_tables(group_queries, codebook)
    pq_scores = score_lists(pq_codes, group_tables, probes, first_list)
    rerank_scores = rerank(queries, vectors, cand_owner, cand_row)
    return (pq_scores, rerank_scores)


def solution(mesh):
    in_specs = (
        P(("group", "shard"), None),
        P(),
        P(("group", "shard"), None, None),
        P("group", None),
        P(("group", "shard"), None),
        P(("group", "shard"), None),
        P(("group", "shard"), None),
    )
    out_specs = (P(("group", "shard"), None, None), P(("group", "shard"), None))
    return jax.shard_map(
        per_device, mesh=mesh, in_specs=in_specs, out_specs=out_specs, check_vma=False
    )
```

profile of v0, /device:TPU:0, one launch (start us, length us, event | category | flops | bytes accessed | tf_op | source)
XLA Modules:
  0.0 161.3 jit_solution(348428554868212641)
XLA Ops:
  5.4 7.5 %all-to-all-start = ((f32[32,1,4]{2,1,0:T(1,128)}), f32[32,1,4]{2,1,0:T(1,128)}, u32[]{:S(2)}, u32[]{:S(2)}) async-start(f32[32,1,4]{2,1,0:T(1,128)} %bitcast.4), calls=%async_computation | async-start | bytes 32768 | tf_op jit(solution)/shard_map/all_to_all | solution.py:60
  12.8 15.7 %all_gather.3 = f32[64,768]{1,0:T(8,128)} all-gather(f32[8,768]{1,0:T(8,128)} %param.9), channel_id=1, replica_groups=mesh['group'=4,'shard'=8] {'shard'}, dimensions={0}, use_global_device_ids=true | all-gather | bytes 221184 | tf_op jit(solution)/shard_map/all_gather | solution.py:73
  28.6 1.1 copy.27
  29.7 7.5 %convert_bitcast_fusion = bf16[96,8,8,256]{3,2,1,0:T(8,128)(2,1)} fusion(f32[96,256,8]{1,2,0:T(8,128)} %param.10, f32[64,768]{0,1:T(8,128)S(1)} %copy.27), kind=kOutput, calls=%fused_computation.13 | convolution fusion | flops 152567808 | bytes 4128768 | tf_op jit(solution)/shard_map/qmd,mkd->qmk/dot_general | solution.py:14
  37.2 3.8 %copy.40 = bf16[96,8,8,256]{3,2,0,1:T(8,128)(2,1)} copy(bf16[96,8,8,256]{3,2,1,0:T(8,128)(2,1)} %convert_bitcast_fusion) | data formatting | bytes 6291456 | tf_op jit(solution)/shard_map/convert_element_type | solution.py:15
  41.0 3.0 %scatter_custom_fusion.1 = f32[128,768]{1,0:T(8,128)S(1)} fusion(s32[128]{0:T(128)S(1)} %fusion.10, f32[8,768]{1,0:T(8,128)} %param.9, s32[1024]{0:T(1024)S(1)} %pad_clamp_fusion.2, f32[]{:T(128)} %constant.28.clone.1), kind=kCustom, calls=%fused_computation.16 | custom fusion | bytes 393728 | tf_op jit(solution)/shard_map/scatter | solution.py:50
  44.8 5.4 %all-to-all-start.1 = ((f32[32,4,768]{2,1,0:T(4,128)}), f32[32,4,768]{2,1,0:T(4,128)S(1)}, u32[]{:S(2)}, u32[]{:S(2)}) async-start(f32[32,4,768]{2,1,0:T(4,128)} %reshape.135), calls=%async_computation.1 | async-start | bytes 786432 | tf_op jit(solution)/shard_map/all_to_all | solution.py:59
  50.3 84.8 %while.11 = (s32[]{:T(128)}, f32[8,256,64]{1,2,0:T(8,128)}, s32[8]{0:T(128)S(1)}, s32[64,8]{0,1:T(8,128)S(1)}, s32[8,96,256]{2,1,0:T(8,128)}, /*index=5*/bf16[64,24576]{1,0:T(8,128)(2,1)}, s32[]{:T(128)}) while((s32[]{:T(128)}, f32[8,256,64]{1,2,0:T(8,128)}, s32[8]{0:T(128)S(1)}, s32[64,8]{0,1:T(8,128)S(1)}, ...), condition=%wide.region_2.3_spmd.clone, body=%wide.region_0.2_spmd.clone.sunk | while | flops 811615168 | bytes 29067528 | solution.py:32
  50.4 1.1 dynamic-slice_bitcast_fusion.2
  51.5 4.3 %bitcast_compare_fusion.2 = pred[24576,256]{1,0:T(32,128)(4,1)S(1)} fusion(s32[24576]{0:T(1024)S(1)} %bitcast.56, s32[96,256]{1,0:T(8,128)S(1)} %dynamic-slice_bitcast_fusion.2), kind=kLoop, calls=%fused_computation.6.clone.1 | loop fusion | flops 6291456 | bytes 6488064 | tf_op jit(solution)/shard_map/while/body/eval_jaxpr/eq | solution.py:23
  57.0 3.9 %fusion.21 = f32[8,256,64]{1,2,0:T(8,128)} fusion(f32[8,256,64]{1,2,0:T(8,128)} %get-tuple-element.111, s32[]{:T(128)S(6)} %copy.46, pred[24576,256]{1,0:T(32,128)(4,1)S(1)} %bitcast_compare_fusion.2, bf16[64,24576]{1,0:T(8,128)(2,1)S(1)} %copy-done.1, pred[64]{0:T(512)(128)(4,1)S(1)} %compare_reduce_fusion.2), kind=kOutput, calls=%fused_computation.9.clone.1 | convolution fusion | flops 805322752 | bytes 9502788 | tf_op jit(solution)/shard_map/while/body/eval_jaxpr/dot_general | solution.py:25
  61.0 1.1 dynamic-slice_bitcast_fusion.2
  62.1 4.3 %bitcast_compare_fusion.2 = pred[24576,256]{1,0:T(32,128)(4,1)S(1)} fusion(s32[24576]{0:T(1024)S(1)} %bitcast.56, s32[96,256]{1,0:T(8,128)S(1)} %dynamic-slice_bitcast_fusion.2), kind=kLoop, calls=%fused_computation.6.clone.1 | loop fusion | flops 6291456 | bytes 6488064 | tf_op jit(solution)/shard_map/while/body/eval_jaxpr/eq | solution.py:23
  67.6 3.9 %fusion.21 = f32[8,256,64]{1,2,0:T(8,128)} fusion(f32[8,256,64]{1,2,0:T(8,128)} %get-tuple-element.111, s32[]{:T(128)S(6)} %copy.46, pred[24576,256]{1,0:T(32,128)(4,1)S(1)} %bitcast_compare_fusion.2, bf16[64,24576]{1,0:T(8,128)(2,1)S(1)} %copy-done.1, pred[64]{0:T(512)(128)(4,1)S(1)} %compare_reduce_fusion.2), kind=kOutput, calls=%fused_computation.9.clone.1 | convolution fusion | flops 805322752 | bytes 9502788 | tf_op jit(solution)/shard_map/while/body/eval_jaxpr/dot_general | solution.py:25
  72.7 4.3 %bitcast_compare_fusion.2 = pred[24576,256]{1,0:T(32,128)(4,1)S(1)} fusion(s32[24576]{0:T(1024)S(1)} %bitcast.56, s32[96,256]{1,0:T(8,128)S(1)} %dynamic-slice_bitcast_fusion.2), kind=kLoop, calls=%fused_computation.6.clone.1 | loop fusion | flops 6291456 | bytes 6488064 | tf_op jit(solution)/shard_map/while/body/eval_jaxpr/eq | solution.py:23
  78.2 3.9 %fusion.21 = f32[8,256,64]{1,2,0:T(8,128)} fusion(f32[8,256,64]{1,2,0:T(8,128)} %get-tuple-element.111, s32[]{:T(128)S(6)} %copy.46, pred[24576,256]{1,0:T(32,128)(4,1)S(1)} %bitcast_compare_fusion.2, bf16[64,24576]{1,0:T(8,128)(2,1)S(1)} %copy-done.1, pred[64]{0:T(512)(128)(4,1)S(1)} %compare_reduce_fusion.2), kind=kOutput, calls=%fused_computation.9.clone.1 | convolution fusion | flops 805322752 | bytes 9502788 | tf_op jit(solution)/shard_map/while/body/eval_jaxpr/dot_general | solution.py:25
  83.3 4.3 %bitcast_compare_fusion.2 = pred[24576,256]{1,0:T(32,128)(4,1)S(1)} fusion(s32[24576]{0:T(1024)S(1)} %bitcast.56, s32[96,256]{1,0:T(8,128)S(1)} %dynamic-slice_bitcast_fusion.2), kind=kLoop, calls=%fused_computation.6.clone.1 | loop fusion | flops 6291456 | bytes 6488064 | tf_op jit(solution)/shard_map/while/body/eval_jaxpr/eq | solution.py:23
  88.8 3.9 %fusion.21 = f32[8,256,64]{1,2,0:T(8,128)} fusion(f32[8,256,64]{1,2,0:T(8,128)} %get-tuple-element.111, s32[]{:T(128)S(6)} %copy.46, pred[24576,256]{1,0:T(32,128)(4,1)S(1)} %bitcast_compare_fusion.2, bf16[64,24576]{1,0:T(8,128)(2,1)S(1)} %copy-done.1, pred[64]{0:T(512)(128)(4,1)S(1)} %compare_reduce_fusion.2), kind=kOutput, calls=%fused_computation.9.clone.1 | convolution fusion | flops 805322752 | bytes 9502788 | tf_op jit(solution)/shard_map/while/body/eval_jaxpr/dot_general | solution.py:25
  93.8 4.3 %bitcast_compare_fusion.2 = pred[24576,256]{1,0:T(32,128)(4,1)S(1)} fusion(s32[24576]{0:T(1024)S(1)} %bitcast.56, s32[96,256]{1,0:T(8,128)S(1)} %dynamic-slice_bitcast_fusion.2), kind=kLoop, calls=%fused_computation.6.clone.1 | loop fusion | flops 6291456 | bytes 6488064 | tf_op jit(solution)/shard_map/while/body/eval_jaxpr/eq | solution.py:23
  99.4 3.9 %fusion.21 = f32[8,256,64]{1,2,0:T(8,128)} fusion(f32[8,256,64]{1,2,0:T(8,128)} %get-tuple-element.111, s32[]{:T(128)S(6)} %copy.46, pred[24576,256]{1,0:T(32,128)(4,1)S(1)} %bitcast_compare_fusion.2, bf16[64,24576]{1,0:T(8,128)(2,1)S(1)} %copy-done.1, pred[64]{0:T(512)(128)(4,1)S(1)} %compare_reduce_fusion.2), kind=kOutput, calls=%fused_computation.9.clone.1 | convolution fusion | flops 805322752 | bytes 9502788 | tf_op jit(solution)/shard_map/while/body/eval_jaxpr/dot_general | solution.py:25
  104.4 4.3 %bitcast_compare_fusion.2 = pred[24576,256]{1,0:T(32,128)(4,1)S(1)} fusion(s32[24576]{0:T(1024)S(1)} %bitcast.56, s32[96,256]{1,0:T(8,128)S(1)} %dynamic-slice_bitcast_fusion.2), kind=kLoop, calls=%fused_computation.6.clone.1 | loop fusion | flops 6291456 | bytes 6488064 | tf_op jit(solution)/shard_map/while/body/eval_jaxpr/eq | solution.py:23
  110.0 3.9 %fusion.21 = f32[8,256,64]{1,2,0:T(8,128)} fusion(f32[8,256,64]{1,2,0:T(8,128)} %get-tuple-element.111, s32[]{:T(128)S(6)} %copy.46, pred[24576,256]{1,0:T(32,128)(4,1)S(1)} %bitcast_compare_fusion.2, bf16[64,24576]{1,0:T(8,128)(2,1)S(1)} %copy-done.1, pred[64]{0:T(512)(128)(4,1)S(1)} %compare_reduce_fusion.2), kind=kOutput, calls=%fused_computation.9.clone.1 | convolution fusion | flops 805322752 | bytes 9502788 | tf_op jit(solution)/shard_map/while/body/eval_jaxpr/dot_general | solution.py:25
  115.0 4.3 %bitcast_compare_fusion.2 = pred[24576,256]{1,0:T(32,128)(4,1)S(1)} fusion(s32[24576]{0:T(1024)S(1)} %bitcast.56, s32[96,256]{1,0:T(8,128)S(1)} %dynamic-slice_bitcast_fusion.2), kind=kLoop, calls=%fused_computation.6.clone.1 | loop fusion | flops 6291456 | bytes 6488064 | tf_op jit(solution)/shard_map/while/body/eval_jaxpr/eq | solution.py:23
  120.6 3.9 %fusion.21 = f32[8,256,64]{1,2,0:T(8,128)} fusion(f32[8,256,64]{1,2,0:T(8,128)} %get-tuple-element.111, s32[]{:T(128)S(6)} %copy.46, pred[24576,256]{1,0:T(32,128)(4,1)S(1)} %bitcast_compare_fusion.2, bf16[64,24576]{1,0:T(8,128)(2,1)S(1)} %copy-done.1, pred[64]{0:T(512)(128)(4,1)S(1)} %compare_reduce_fusion.2), kind=kOutput, calls=%fused_computation.9.clone.1 | convolution fusion | flops 805322752 | bytes 9502788 | tf_op jit(solution)/shard_map/while/body/eval_jaxpr/dot_general | solution.py:25
  125.6 4.3 %bitcast_compare_fusion.2 = pred[24576,256]{1,0:T(32,128)(4,1)S(1)} fusion(s32[24576]{0:T(1024)S(1)} %bitcast.56, s32[96,256]{1,0:T(8,128)S(1)} %dynamic-slice_bitcast_fusion.2), kind=kLoop, calls=%fused_computation.6.clone.1 | loop fusion | flops 6291456 | bytes 6488064 | tf_op jit(solution)/shard_map/while/body/eval_jaxpr/eq | solution.py:23
  131.2 3.9 %fusion.21 = f32[8,256,64]{1,2,0:T(8,128)} fusion(f32[8,256,64]{1,2,0:T(8,128)} %get-tuple-element.111, s32[]{:T(128)S(6)} %copy.46, pred[24576,256]{1,0:T(32,128)(4,1)S(1)} %bitcast_compare_fusion.2, bf16[64,24576]{1,0:T(8,128)(2,1)S(1)} %copy-done.1, pred[64]{0:T(512)(128)(4,1)S(1)} %compare_reduce_fusion.2), kind=kOutput, calls=%fused_computation.9.clone.1 | convolution fusion | flops 805322752 | bytes 9502788 | tf_op jit(solution)/shard_map/while/body/eval_jaxpr/dot_general | solution.py:25
  139.1 1.6 gather_fusion
  140.7 1.8 %reshape.147 = f32[32,4,768]{2,1,0:T(4,128)} reshape(f32[128,768]{1,0:T(8,128)} %gather_fusion) | data formatting | bytes 786432 | tf_op jit(solution)/shard_map/gather | solution.py:63
  142.5 1.2 multiply_reduce_fusion
  145.1 5.8 %all-to-all-start.2 = ((f32[32,1,4]{2,1,0:T(1,128)}), f32[32,1,4]{2,1,0:T(1,128)S(1)}, u32[]{:S(2)}, u32[]{:S(2)}) async-start(f32[32,1,4]{2,1,0:T(1,128)} %copy.33), calls=%async_computation.2 | async-start | bytes 32768 | tf_op jit(solution)/shard_map/all_to_all | solution.py:66
  151.6 6.5 %all-to-all-done.2 = f32[32,1,4]{2,1,0:T(1,128)S(1)} async-done(((f32[32,1,4]{2,1,0:T(1,128)}), f32[32,1,4]{2,1,0:T(1,128)S(1)}, u32[]{:S(2)}, u32[]{:S(2)}) %all-to-all-start.2) | async-done | bytes 544 | tf_op jit(solution)/shard_map/all_to_all | solution.py:66
  159.4 1.2 gather_fusion.1
  (93 shorter events, 30.7 us)
Async XLA Ops:
  0.6 138.5 %copy-start = (f32[1024,768]{1,0:T(8,128)S(1)}, f32[1024,768]{1,0:T(8,128)}, u32[]{:S(2)}) copy-start(f32[1024,768]{1,0:T(8,128)} %param.13) | copy-start | bytes 9437188
  3.7 41.2 %copy-start.4 = (s32[128]{0:T(128)}, s32[128]{0:T(128)S(1)}, u32[]{:S(2)}) copy-start(s32[128]{0:T(128)S(1)} %fusion.10) | copy-start | bytes 1540
  5.4 39.5 %all-to-all-start = ((f32[32,1,4]{2,1,0:T(1,128)}), f32[32,1,4]{2,1,0:T(1,128)}, u32[]{:S(2)}, u32[]{:S(2)}) async-start(f32[32,1,4]{2,1,0:T(1,128)} %bitcast.4), calls=%async_computation | async-start | bytes 32768 | tf_op jit(solution)/shard_map/all_to_all | solution.py:60
  29.7 20.6 %copy-start.2 = (s32[64,8]{0,1:T(8,128)S(1)}, s32[64,8]{0,1:T(8,128)}, u32[]{:S(2)}) copy-start(s32[64,8]{0,1:T(8,128)} %param.12) | copy-start | bytes 6148
  44.8 97.7 %all-to-all-start.1 = ((f32[32,4,768]{2,1,0:T(4,128)}), f32[32,4,768]{2,1,0:T(4,128)S(1)}, u32[]{:S(2)}, u32[]{:S(2)}) async-start(f32[32,4,768]{2,1,0:T(4,128)} %reshape.135), calls=%async_computation.1 | async-start | bytes 786432 | tf_op jit(solution)/shard_map/all_to_all | solution.py:59
  50.3 6.7 %copy-start.1 = (bf16[64,24576]{1,0:T(8,128)(2,1)S(1)}, bf16[64,24576]{1,0:T(8,128)(2,1)}, u32[]{:S(2)}) copy-start(bf16[64,24576]{1,0:T(8,128)(2,1)} %get-tuple-element.122) | copy-start | bytes 9437188 | tf_op jit(solution)/shard_map/while
  60.9 6.7 %copy-start.1 = (bf16[64,24576]{1,0:T(8,128)(2,1)S(1)}, bf16[64,24576]{1,0:T(8,128)(2,1)}, u32[]{:S(2)}) copy-start(bf16[64,24576]{1,0:T(8,128)(2,1)} %get-tuple-element.122) | copy-start | bytes 9437188 | tf_op jit(solution)/shard_map/while
  71.5 6.7 %copy-start.1 = (bf16[64,24576]{1,0:T(8,128)(2,1)S(1)}, bf16[64,24576]{1,0:T(8,128)(2,1)}, u32[]{:S(2)}) copy-start(bf16[64,24576]{1,0:T(8,128)(2,1)} %get-tuple-element.122) | copy-start | bytes 9437188 | tf_op jit(solution)/shard_map/while
  82.1 6.7 %copy-start.1 = (bf16[64,24576]{1,0:T(8,128)(2,1)S(1)}, bf16[64,24576]{1,0:T(8,128)(2,1)}, u32[]{:S(2)}) copy-start(bf16[64,24576]{1,0:T(8,128)(2,1)} %get-tuple-element.122) | copy-start | bytes 9437188 | tf_op jit(solution)/shard_map/while
  92.7 6.7 %copy-start.1 = (bf16[64,24576]{1,0:T(8,128)(2,1)S(1)}, bf16[64,24576]{1,0:T(8,128)(2,1)}, u32[]{:S(2)}) copy-start(bf16[64,24576]{1,0:T(8,128)(2,1)} %get-tuple-element.122) | copy-start | bytes 9437188 | tf_op jit(solution)/shard_map/while
  103.3 6.7 %copy-start.1 = (bf16[64,24576]{1,0:T(8,128)(2,1)S(1)}, bf16[64,24576]{1,0:T(8,128)(2,1)}, u32[]{:S(2)}) copy-start(bf16[64,24576]{1,0:T(8,128)(2,1)} %get-tuple-element.122) | copy-start | bytes 9437188 | tf_op jit(solution)/shard_map/while
  113.9 6.7 %copy-start.1 = (bf16[64,24576]{1,0:T(8,128)(2,1)S(1)}, bf16[64,24576]{1,0:T(8,128)(2,1)}, u32[]{:S(2)}) copy-start(bf16[64,24576]{1,0:T(8,128)(2,1)} %get-tuple-element.122) | copy-start | bytes 9437188 | tf_op jit(solution)/shard_map/while
  124.5 6.7 %copy-start.1 = (bf16[64,24576]{1,0:T(8,128)(2,1)S(1)}, bf16[64,24576]{1,0:T(8,128)(2,1)}, u32[]{:S(2)}) copy-start(bf16[64,24576]{1,0:T(8,128)(2,1)} %get-tuple-element.122) | copy-start | bytes 9437188 | tf_op jit(solution)/shard_map/while
  135.9 0.6 copy-start.3
  145.1 13.0 %all-to-all-start.2 = ((f32[32,1,4]{2,1,0:T(1,128)}), f32[32,1,4]{2,1,0:T(1,128)S(1)}, u32[]{:S(2)}, u32[]{:S(2)}) async-start(f32[32,1,4]{2,1,0:T(1,128)} %copy.33), calls=%async_computation.2 | async-start | bytes 32768 | tf_op jit(solution)/shard_map/all_to_all | solution.py:66
where the time goes:
time: 162 us; the launch traced here: 161 us
  other arithmetic  45.8 us (28%)
  matrix products  38.9 us (24%)
  local copies, waits for them, and re-layouts  34.8 us (21%)
  starting transfers between devices  18.7 us (12%)
  blocking collectives  15.7 us (10%)
  waiting for transfers between devices  6.5 us (4%)
    eq x8, other arithmetic, one_list(): list_codes[:, None, :] == centres[None, :, None]  34.1 us
    dot_general x8, matrix products, one_list(): lax.dot_general(onehot, group_tables, (((0,), (1,)), ((), ())), preferred...  31.3 us
    all_gather x1, blocking collectives, per_device(): group_queries = lax.all_gather(queries, 'shard', axis=0, tiled=True)  15.7 us
    eq x8, local copies, waits for them, and re-layouts, one_list(): list_codes[:, None, :] == centres[None, :, None]  8.45 us
    dot_general x1, matrix products, build_tables(): jnp.einsum('qmd,mkd->qmk', pieces, codebook, precision=lax.Precision.HIGH...  7.55 us
    all_to_all x1, starting transfers between devices, rerank(): lax.all_to_all(send_ids, ('group', 'shard'), split_axis=0, concat_axis=0,...  7.45 us
    all_to_all x1, waiting for transfers between devices, rerank(): lax.all_to_all(scored, ('group', 'shard'), split_axis=0, concat_axis=0, t...  6.49 us
    all_to_all x1, starting transfers between devices, rerank(): lax.all_to_all(scored, ('group', 'shard'), split_axis=0, concat_axis=0, t...  5.83 us
  transfers between devices with their start and end apart: 3, of which 1 were waited for; matrix products, arithmetic and copies ran while one was open for 67% of the time, Pallas kernels for 0%

commit v1 on v0

--- a/solution.py
+++ b/solution.py
@@ -6,6 +6,15 @@
 M = 96
 DS = 8
 KS = 256
+
+
+def report_samples_up(content):
+    device_axis = "shard"
+    size_here = jax.lax.axis_size(device_axis)
+    stack_in = [size_here if num == 0 else 1 for num in range(content.ndim)]
+    return jax.lax.all_to_all(
+        jnp.tile(content, stack_in), device_axis, split_axis=0, concat_axis=0, tiled=True
+    )
 
 
 def build_tables(query_rows, codebook):
@@ -70,7 +79,7 @@
 
 def per_device(queries, codebook, pq_codes, probes, vectors, cand_owner, cand_row):
     first_list = lax.axis_index("shard") * pq_codes.shape[0]
-    group_queries = lax.all_gather(queries, "shard", axis=0, tiled=True)
+    group_queries = report_samples_up(queries)
     group_tables = build_tables(group_queries, codebook)
     pq_scores = score_lists(pq_codes, group_tables, probes, first_list)
     rerank_scores = rerank(queries, vectors, cand_owner, cand_row)

time: 162 us -> 157 us (0.969)
  starting transfers between devices: 18.7 us -> 12.6 us
  waiting for transfers between devices: 6.5 us -> 3.46 us
  other arithmetic: 45.8 us -> 48.4 us
    all_gather x1 -> x0, blocking collectives: 15.7 us -> none  [per_device(): group_queries = lax.all_gather(queries, 'shard', axis=0, tiled=True)]
    all_to_all x0 -> x1, blocking collectives: none -> 14.3 us  [rerank(): lax.all_to_all(send_ids, ('group', 'shard'), split_axis=0, concat_axis=0,...]
    all_to_all x1, waiting for transfers between devices: 6.49 us -> 0.01 us  [rerank(): lax.all_to_all(scored, ('group', 'shard'), split_axis=0, concat_axis=0, t...]
    reshape x0 -> x1, local copies, waits for them, and re-layouts: none -> 3.86 us  [build_tables(): pieces = query_rows.reshape(number, M, DS)]
    all_to_all x1, waiting for transfers between devices: 0.01 us -> 3.45 us  [report_samples_up(): jax.lax.all_to_all(jnp.tile(content, stack_in), device_axis, split_axis=0...]
    all_to_all x1, starting transfers between devices: 7.45 us -> 4.02 us  [report_samples_up(): jax.lax.all_to_all(jnp.tile(content, stack_in), device_axis, split_axis=0...]
    all_to_all x1, starting transfers between devices: 5.45 us -> 2.59 us  [rerank(): lax.all_to_all(send_rows, ('group', 'shard'), split_axis=0, concat_axis=0...]
    convert_element_type x1, local copies, waits for them, and re-layouts: 3.76 us -> 1.87 us  [build_tables(): return tables.reshape(number, M * KS).astype(jnp.bfloat16)]
  transfers between devices with their start and end apart: 3 -> 3, of which waited for: 1 -> 1; matrix products, arithmetic and copies ran while one was open for 67% -> 72% of each run, Pallas kernels for 0% -> 0%
where the time goes in v1:
time: 157 us; the launch traced here: 156 us
  other arithmetic  48.4 us (31%)
  matrix products  40 us (25%)
  local copies, waits for them, and re-layouts  36.3 us (23%)
  blocking collectives  14.3 us (9%)
  starting transfers between devices  12.6 us (8%)
  waiting for transfers between devices  3.46 us (2%)
    eq x8, other arithmetic, one_list(): list_codes[:, None, :] == centres[None, :, None]  34.6 us
    dot_general x8, matrix products, one_list(): lax.dot_general(onehot, group_tables, (((0,), (1,)), ((), ())), preferred...  31.3 us
    all_to_all x1, blocking collectives, rerank(): lax.all_to_all(send_ids, ('group', 'shard'), split_axis=0, concat_axis=0,...  14.3 us
    dot_general x1, matrix products, build_tables(): jnp.einsum('qmd,mkd->qmk', pieces, codebook, precision=lax.Precision.HIGH...  8.7 us
    eq x8, local copies, waits for them, and re-layouts, one_list(): list_codes[:, None, :] == centres[None, :, None]  7.25 us
    all_to_all x1, starting transfers between devices, rerank(): lax.all_to_all(scored, ('group', 'shard'), split_axis=0, concat_axis=0, t...  6.01 us
    reduce_or x8, other arithmetic, one_list(): probed = jnp.any(probes == list_id, axis=1)  5.11 us
    dynamic_slice x8, local copies, waits for them, and re-layouts, score_lists(): return lax.map(one_list, (pq_codes, list_ids))  4.8 us
  transfers between devices with their start and end apart: 3, of which 1 were waited for; matrix products, arithmetic and copies ran while one was open for 72% of the time, Pallas kernels for 0%

profile of v1, /device:TPU:0, one launch (start us, length us, event | category | flops | bytes accessed | tf_op | source)
XLA Modules:
  0.0 156.1 jit_solution(7410046930991553723)
XLA Ops:
  5.3 14.3 %all_to_all.29 = f32[32,1,4]{2,1,0:T(1,128)S(1)} all-to-all(f32[32,1,4]{2,1,0:T(1,128)S(1)} %bitcast.54), channel_id=1, replica_groups=mesh['group'=4,'shard'=8] {'group','shard'}, dimensions={0} | all-to-all | bytes 1024 | tf_op jit(solution)/shard_map/all_to_all | solution.py:69
  19.6 1.4 tile.2
  21.1 4.0 %all-to-all-start = ((f32[8,8,768]{2,1,0:T(8,128)}), f32[8,8,768]{2,1,0:T(8,128)}, u32[]{:S(2)}, u32[]{:S(2)}) async-start(f32[8,8,768]{2,1,0:T(8,128)} %tile.2), calls=%async_computation | async-start | bytes 393216 | tf_op jit(solution)/shard_map/all_to_all | solution.py:15
  25.7 3.4 %scatter_custom_fusion.1 = f32[128,768]{1,0:T(8,128)S(1)} fusion(s32[128]{0:T(128)} %copy-done.4, f32[8,768]{1,0:T(8,128)} %param.9, s32[1024]{0:T(1024)} %pad_clamp_fusion.2, f32[]{:T(128)} %constant.28.clone.1), kind=kCustom, calls=%fused_computation.17 | custom fusion | bytes 393728 | tf_op jit(solution)/shard_map/scatter | solution.py:59
  29.9 3.5 %all-to-all-done = f32[8,8,768]{2,1,0:T(8,128)} async-done(((f32[8,8,768]{2,1,0:T(8,128)}), f32[8,8,768]{2,1,0:T(8,128)}, u32[]{:S(2)}, u32[]{:S(2)}) %all-to-all-start) | async-done | bytes 196640 | tf_op jit(solution)/shard_map/all_to_all | solution.py:15
  33.4 2.6 %all-to-all-start.2 = ((f32[32,4,768]{2,1,0:T(4,128)}), f32[32,4,768]{2,1,0:T(4,128)S(1)}, u32[]{:S(2)}, u32[]{:S(2)}) async-start(f32[32,4,768]{2,1,0:T(4,128)} %reshape.143), calls=%async_computation.2 | async-start | bytes 786432 | tf_op jit(solution)/shard_map/all_to_all | solution.py:68
  38.4 1.3 compare_select_fusion
  41.7 1.5 gather_fusion
  43.2 1.8 %reshape.155 = f32[32,4,768]{2,1,0:T(4,128)} reshape(f32[128,768]{1,0:T(8,128)} %gather_fusion) | data formatting | bytes 786432 | tf_op jit(solution)/shard_map/gather | solution.py:72
  45.1 3.9 %reshape.142 = f32[64,96,8]{2,1,0:T(8,128)} reshape(f32[8,8,768]{2,1,0:T(8,128)} %all-to-all-done) | data formatting | bytes 393216 | tf_op jit(solution)/shard_map/reshape | solution.py:22
  48.9 8.7 %convert_bitcast_fusion = bf16[96,8,8,256]{3,2,1,0:T(8,128)(2,1)S(1)} fusion(f32[96,256,8]{1,2,0:T(8,128)} %param.10, f32[64,96,8]{2,1,0:T(8,128)} %reshape.142), kind=kOutput, calls=%fused_computation.15 | convolution fusion | flops 152567808 | bytes 4128768 | tf_op jit(solution)/shard_map/qmd,mkd->qmk/dot_general | solution.py:23
  57.7 1.9 %copy.40 = bf16[96,8,8,256]{3,2,0,1:T(8,128)(2,1)} copy(bf16[96,8,8,256]{3,2,1,0:T(8,128)(2,1)S(1)} %convert_bitcast_fusion) | data formatting | bytes 6291456 | tf_op jit(solution)/shard_map/convert_element_type | solution.py:24
  59.6 1.8 %multiply_reduce_fusion = f32[32,4]{1,0:T(8,128)} fusion(f32[32,4,768]{2,1,0:T(4,128)S(1)} %all-to-all-done.2, f32[32,4,768]{2,1,0:T(4,128)} %reshape.155), kind=kLoop, calls=%fused_computation.16 | loop fusion | flops 196480 | bytes 786944
  62.8 6.0 %all-to-all-start.3 = ((f32[32,1,4]{2,1,0:T(1,128)}), f32[32,1,4]{2,1,0:T(1,128)S(1)}, u32[]{:S(2)}, u32[]{:S(2)}) async-start(f32[32,1,4]{2,1,0:T(1,128)} %copy.33), calls=%async_computation.3 | async-start | bytes 32768 | tf_op jit(solution)/shard_map/all_to_all | solution.py:75
  68.9 83.8 %while.11 = (s32[]{:T(128)}, f32[8,256,64]{1,2,0:T(8,128)}, s32[8]{0:T(128)S(1)}, s32[64,8]{0,1:T(8,128)S(1)}, s32[8,96,256]{2,1,0:T(8,128)}, /*index=5*/bf16[64,24576]{1,0:T(8,128)(2,1)}, s32[]{:T(128)}) while((s32[]{:T(128)}, f32[8,256,64]{1,2,0:T(8,128)}, s32[8]{0:T(128)S(1)}, s32[64,8]{0,1:T(8,128)S(1)}, ...), condition=%wide.region_2.3_spmd.clone, body=%wide.region_0.2_spmd.clone.sunk | while | flops 811615168 | bytes 29067528 | solution.py:41
  69.9 4.3 %bitcast_compare_fusion.2 = pred[24576,256]{1,0:T(32,128)(4,1)S(1)} fusion(s32[24576]{0:T(1024)S(1)} %bitcast.53, s32[96,256]{1,0:T(8,128)S(1)} %dynamic-slice_bitcast_fusion.2), kind=kLoop, calls=%fused_computation.6.clone.1 | loop fusion | flops 6291456 | bytes 6488064 | tf_op jit(solution)/shard_map/while/body/eval_jaxpr/eq | solution.py:32
  75.4 3.9 %fusion.24 = f32[8,256,64]{1,2,0:T(8,128)} fusion(f32[8,256,64]{1,2,0:T(8,128)} %get-tuple-element.111, s32[]{:T(128)S(6)} %copy.50, pred[24576,256]{1,0:T(32,128)(4,1)S(1)} %bitcast_compare_fusion.2, bf16[64,24576]{1,0:T(8,128)(2,1)S(1)} %copy-done.1, pred[64]{0:T(512)(128)(4,1)S(1)} %compare_reduce_fusion.2), kind=kOutput, calls=%fused_computation.9.clone.1 | convolution fusion | flops 805322752 | bytes 9502788 | tf_op jit(solution)/shard_map/while/body/eval_jaxpr/dot_general | solution.py:34
  80.3 4.3 %bitcast_compare_fusion.2 = pred[24576,256]{1,0:T(32,128)(4,1)S(1)} fusion(s32[24576]{0:T(1024)S(1)} %bitcast.53, s32[96,256]{1,0:T(8,128)S(1)} %dynamic-slice_bitcast_fusion.2), kind=kLoop, calls=%fused_computation.6.clone.1 | loop fusion | flops 6291456 | bytes 6488064 | tf_op jit(solution)/shard_map/while/body/eval_jaxpr/eq | solution.py:32
  85.9 3.9 %fusion.24 = f32[8,256,64]{1,2,0:T(8,128)} fusion(f32[8,256,64]{1,2,0:T(8,128)} %get-tuple-element.111, s32[]{:T(128)S(6)} %copy.50, pred[24576,256]{1,0:T(32,128)(4,1)S(1)} %bitcast_compare_fusion.2, bf16[64,24576]{1,0:T(8,128)(2,1)S(1)} %copy-done.1, pred[64]{0:T(512)(128)(4,1)S(1)} %compare_reduce_fusion.2), kind=kOutput, calls=%fused_computation.9.clone.1 | convolution fusion | flops 805322752 | bytes 9502788 | tf_op jit(solution)/shard_map/while/body/eval_jaxpr/dot_general | solution.py:34
  90.8 4.3 %bitcast_compare_fusion.2 = pred[24576,256]{1,0:T(32,128)(4,1)S(1)} fusion(s32[24576]{0:T(1024)S(1)} %bitcast.53, s32[96,256]{1,0:T(8,128)S(1)} %dynamic-slice_bitcast_fusion.2), kind=kLoop, calls=%fused_computation.6.clone.1 | loop fusion | flops 6291456 | bytes 6488064 | tf_op jit(solution)/shard_map/while/body/eval_jaxpr/eq | solution.py:32
  96.4 3.9 %fusion.24 = f32[8,256,64]{1,2,0:T(8,128)} fusion(f32[8,256,64]{1,2,0:T(8,128)} %get-tuple-element.111, s32[]{:T(128)S(6)} %copy.50, pred[24576,256]{1,0:T(32,128)(4,1)S(1)} %bitcast_compare_fusion.2, bf16[64,24576]{1,0:T(8,128)(2,1)S(1)} %copy-done.1, pred[64]{0:T(512)(128)(4,1)S(1)} %compare_reduce_fusion.2), kind=kOutput, calls=%fused_computation.9.clone.1 | convolution fusion | flops 805322752 | bytes 9502788 | tf_op jit(solution)/shard_map/while/body/eval_jaxpr/dot_general | solution.py:34
  101.3 4.3 %bitcast_compare_fusion.2 = pred[24576,256]{1,0:T(32,128)(4,1)S(1)} fusion(s32[24576]{0:T(1024)S(1)} %bitcast.53, s32[96,256]{1,0:T(8,128)S(1)} %dynamic-slice_bitcast_fusion.2), kind=kLoop, calls=%fused_computation.6.clone.1 | loop fusion | flops 6291456 | bytes 6488064 | tf_op jit(solution)/shard_map/while/body/eval_jaxpr/eq | solution.py:32
  106.8 3.9 %fusion.24 = f32[8,256,64]{1,2,0:T(8,128)} fusion(f32[8,256,64]{1,2,0:T(8,128)} %get-tuple-element.111, s32[]{:T(128)S(6)} %copy.50, pred[24576,256]{1,0:T(32,128)(4,1)S(1)} %bitcast_compare_fusion.2, bf16[64,24576]{1,0:T(8,128)(2,1)S(1)} %copy-done.1, pred[64]{0:T(512)(128)(4,1)S(1)} %compare_reduce_fusion.2), kind=kOutput, calls=%fused_computation.9.clone.1 | convolution fusion | flops 805322752 | bytes 9502788 | tf_op jit(solution)/shard_map/while/body/eval_jaxpr/dot_general | solution.py:34
  111.7 4.3 %bitcast_compare_fusion.2 = pred[24576,256]{1,0:T(32,128)(4,1)S(1)} fusion(s32[24576]{0:T(1024)S(1)} %bitcast.53, s32[96,256]{1,0:T(8,128)S(1)} %dynamic-slice_bitcast_fusion.2), kind=kLoop, calls=%fused_computation.6.clone.1 | loop fusion | flops 6291456 | bytes 6488064 | tf_op jit(solution)/shard_map/while/body/eval_jaxpr/eq | solution.py:32
  117.3 3.9 %fusion.24 = f32[8,256,64]{1,2,0:T(8,128)} fusion(f32[8,256,64]{1,2,0:T(8,128)} %get-tuple-element.111, s32[]{:T(128)S(6)} %copy.50, pred[24576,256]{1,0:T(32,128)(4,1)S(1)} %bitcast_compare_fusion.2, bf16[64,24576]{1,0:T(8,128)(2,1)S(1)} %copy-done.1, pred[64]{0:T(512)(128)(4,1)S(1)} %compare_reduce_fusion.2), kind=kOutput, calls=%fused_computation.9.clone.1 | convolution fusion | flops 805322752 | bytes 9502788 | tf_op jit(solution)/shard_map/while/body/eval_jaxpr/dot_general | solution.py:34
  122.2 4.3 %bitcast_compare_fusion.2 = pred[24576,256]{1,0:T(32,128)(4,1)S(1)} fusion(s32[24576]{0:T(1024)S(1)} %bitcast.53, s32[96,256]{1,0:T(8,128)S(1)} %dynamic-slice_bitcast_fusion.2), kind=kLoop, calls=%fused_computation.6.clone.1 | loop fusion | flops 6291456 | bytes 6488064 | tf_op jit(solution)/shard_map/while/body/eval_jaxpr/eq | solution.py:32
  127.8 3.9 %fusion.24 = f32[8,256,64]{1,2,0:T(8,128)} fusion(f32[8,256,64]{1,2,0:T(8,128)} %get-tuple-element.111, s32[]{:T(128)S(6)} %copy.50, pred[24576,256]{1,0:T(32,128)(4,1)S(1)} %bitcast_compare_fusion.2, bf16[64,24576]{1,0:T(8,128)(2,1)S(1)} %copy-done.1, pred[64]{0:T(512)(128)(4,1)S(1)} %compare_reduce_fusion.2), kind=kOutput, calls=%fused_computation.9.clone.1 | convolution fusion | flops 805322752 | bytes 9502788 | tf_op jit(solution)/shard_map/while/body/eval_jaxpr/dot_general | solution.py:34
  132.7 4.3 %bitcast_compare_fusion.2 = pred[24576,256]{1,0:T(32,128)(4,1)S(1)} fusion(s32[24576]{0:T(1024)S(1)} %bitcast.53, s32[96,256]{1,0:T(8,128)S(1)} %dynamic-slice_bitcast_fusion.2), kind=kLoop, calls=%fused_computation.6.clone.1 | loop fusion | flops 6291456 | bytes 6488064 | tf_op jit(solution)/shard_map/while/body/eval_jaxpr/eq | solution.py:32
  138.3 3.9 %fusion.24 = f32[8,256,64]{1,2,0:T(8,128)} fusion(f32[8,256,64]{1,2,0:T(8,128)} %get-tuple-element.111, s32[]{:T(128)S(6)} %copy.50, pred[24576,256]{1,0:T(32,128)(4,1)S(1)} %bitcast_compare_fusion.2, bf16[64,24576]{1,0:T(8,128)(2,1)S(1)} %copy-done.1, pred[64]{0:T(512)(128)(4,1)S(1)} %compare_reduce_fusion.2), kind=kOutput, calls=%fused_computation.9.clone.1 | convolution fusion | flops 805322752 | bytes 9502788 | tf_op jit(solution)/shard_map/while/body/eval_jaxpr/dot_general | solution.py:34
  143.1 4.3 %bitcast_compare_fusion.2 = pred[24576,256]{1,0:T(32,128)(4,1)S(1)} fusion(s32[24576]{0:T(1024)S(1)} %bitcast.53, s32[96,256]{1,0:T(8,128)S(1)} %dynamic-slice_bitcast_fusion.2), kind=kLoop, calls=%fused_computation.6.clone.1 | loop fusion | flops 6291456 | bytes 6488064 | tf_op jit(solution)/shard_map/while/body/eval_jaxpr/eq | solution.py:32
  148.7 3.9 %fusion.24 = f32[8,256,64]{1,2,0:T(8,128)} fusion(f32[8,256,64]{1,2,0:T(8,128)} %get-tuple-element.111, s32[]{:T(128)S(6)} %copy.50, pred[24576,256]{1,0:T(32,128)(4,1)S(1)} %bitcast_compare_fusion.2, bf16[64,24576]{1,0:T(8,128)(2,1)S(1)} %copy-done.1, pred[64]{0:T(512)(128)(4,1)S(1)} %compare_reduce_fusion.2), kind=kOutput, calls=%fused_computation.9.clone.1 | convolution fusion | flops 805322752 | bytes 9502788 | tf_op jit(solution)/shard_map/while/body/eval_jaxpr/dot_general | solution.py:34
  154.1 1.4 gather_fusion.1
  (96 shorter events, 31.8 us)
Async XLA Ops:
  0.6 41.1 %copy-start = (f32[1024,768]{1,0:T(8,128)S(1)}, f32[1024,768]{1,0:T(8,128)}, u32[]{:S(2)}) copy-start(f32[1024,768]{1,0:T(8,128)} %param.13) | copy-start | bytes 9437188
  3.7 0.6 copy-start.4
  21.1 12.3 %all-to-all-start = ((f32[8,8,768]{2,1,0:T(8,128)}), f32[8,8,768]{2,1,0:T(8,128)}, u32[]{:S(2)}, u32[]{:S(2)}) async-start(f32[8,8,768]{2,1,0:T(8,128)} %tile.2), calls=%async_computation | async-start | bytes 393216 | tf_op jit(solution)/shard_map/all_to_all | solution.py:15
  33.4 26.2 %all-to-all-start.2 = ((f32[32,4,768]{2,1,0:T(4,128)}), f32[32,4,768]{2,1,0:T(4,128)S(1)}, u32[]{:S(2)}, u32[]{:S(2)}) async-start(f32[32,4,768]{2,1,0:T(4,128)} %reshape.143), calls=%async_computation.2 | async-start | bytes 786432 | tf_op jit(solution)/shard_map/all_to_all | solution.py:68
  57.7 4.5 %copy-start.3 = (f32[32,1,4]{0,2,1:T(4,128)S(1)}, f32[32,1,4]{0,2,1:T(4,128)}, u32[]{:S(2)}) copy-start(f32[32,1,4]{0,2,1:T(4,128)} %copy.30) | copy-start | bytes 1540
  57.7 11.2 %copy-start.2 = (s32[64,8]{0,1:T(8,128)S(1)}, s32[64,8]{0,1:T(8,128)}, u32[]{:S(2)}) copy-start(s32[64,8]{0,1:T(8,128)} %param.12) | copy-start | bytes 6148
  57.7 11.2 %copy-start.5 = (s32[8]{0:T(128)S(1)}, s32[8]{0:T(128)}, u32[]{:S(2)}) copy-start(s32[8]{0:T(128)} %iota_add_fusion) | copy-start | bytes 100
  62.8 89.8 %all-to-all-start.3 = ((f32[32,1,4]{2,1,0:T(1,128)}), f32[32,1,4]{2,1,0:T(1,128)S(1)}, u32[]{:S(2)}, u32[]{:S(2)}) async-start(f32[32,1,4]{2,1,0:T(1,128)} %copy.33), calls=%async_computation.3 | async-start | bytes 32768 | tf_op jit(solution)/shard_map/all_to_all | solution.py:75
  69.8 5.6 %copy-start.1 = (bf16[64,24576]{1,0:T(8,128)(2,1)S(1)}, bf16[64,24576]{1,0:T(8,128)(2,1)}, u32[]{:S(2)}) copy-start(bf16[64,24576]{1,0:T(8,128)(2,1)} %get-tuple-element.122) | copy-start | bytes 9437188 | tf_op jit(solution)/shard_map/while
  80.3 5.6 %copy-start.1 = (bf16[64,24576]{1,0:T(8,128)(2,1)S(1)}, bf16[64,24576]{1,0:T(8,128)(2,1)}, u32[]{:S(2)}) copy-start(bf16[64,24576]{1,0:T(8,128)(2,1)} %get-tuple-element.122) | copy-start | bytes 9437188 | tf_op jit(solution)/shard_map/while
  90.8 5.6 %copy-start.1 = (bf16[64,24576]{1,0:T(8,128)(2,1)S(1)}, bf16[64,24576]{1,0:T(8,128)(2,1)}, u32[]{:S(2)}) copy-start(bf16[64,24576]{1,0:T(8,128)(2,1)} %get-tuple-element.122) | copy-start | bytes 9437188 | tf_op jit(solution)/shard_map/while
  101.3 5.6 %copy-start.1 = (bf16[64,24576]{1,0:T(8,128)(2,1)S(1)}, bf16[64,24576]{1,0:T(8,128)(2,1)}, u32[]{:S(2)}) copy-start(bf16[64,24576]{1,0:T(8,128)(2,1)} %get-tuple-element.122) | copy-start | bytes 9437188 | tf_op jit(solution)/shard_map/while
  111.7 5.6 %copy-start.1 = (bf16[64,24576]{1,0:T(8,128)(2,1)S(1)}, bf16[64,24576]{1,0:T(8,128)(2,1)}, u32[]{:S(2)}) copy-start(bf16[64,24576]{1,0:T(8,128)(2,1)} %get-tuple-element.122) | copy-start | bytes 9437188 | tf_op jit(solution)/shard_map/while
  122.2 5.6 %copy-start.1 = (bf16[64,24576]{1,0:T(8,128)(2,1)S(1)}, bf16[64,24576]{1,0:T(8,128)(2,1)}, u32[]{:S(2)}) copy-start(bf16[64,24576]{1,0:T(8,128)(2,1)} %get-tuple-element.122) | copy-start | bytes 9437188 | tf_op jit(solution)/shard_map/while
  132.7 5.6 %copy-start.1 = (bf16[64,24576]{1,0:T(8,128)(2,1)S(1)}, bf16[64,24576]{1,0:T(8,128)(2,1)}, u32[]{:S(2)}) copy-start(bf16[64,24576]{1,0:T(8,128)(2,1)} %get-tuple-element.122) | copy-start | bytes 9437188 | tf_op jit(solution)/shard_map/while
  143.1 5.6 %copy-start.1 = (bf16[64,24576]{1,0:T(8,128)(2,1)S(1)}, bf16[64,24576]{1,0:T(8,128)(2,1)}, u32[]{:S(2)}) copy-start(bf16[64,24576]{1,0:T(8,128)(2,1)} %get-tuple-element.122) | copy-start | bytes 9437188 | tf_op jit(solution)/shard_map/while
